TPU v7x, 256 devices: a whole 4x4x8 slice. The times are simulated.
256 devices in a mesh: strata: 16 (over z_lo, x), users: 16 (over y, z_hi, core).
Axes of the slice: x: 4, y: 4, z: 8 (z_hi: 2, z_lo: 4; z = z_hi * 4 + z_lo), core: 2. Of those that a mesh axis runs over, the one named last changes fastest.
Arguments:
- user_factors: float32 [524288, 256], P(('strata', 'users')), may hold values from -1.5 to 1.5
- item_factors: float32 [16384, 256], P(('strata', 'users')), may hold values from -1.5 to 1.5
- tile_rows: int32 [16, 16, 2, 64], P('strata', 'users'), may hold values from 0 to 15, as said below
- tile_columns: int32 [16, 16, 2, 64], P('strata', 'users'), may hold values from 0 to 7, as said below
- tile_counts: int32 [16, 16, 2], P('strata', 'users'), may hold values from 8 to 64, as said below
- ratings: int32 [16, 16, 2, 64, 128, 128], P('strata', 'users'), may hold values from 0 to 5
Outputs:
- updated_users: float32 [524288, 256], P(('strata', 'users'))
- updated_items: float32 [16384, 256], P(('strata', 'users'))
Inputs may be any that keep to these rules, and one draw needn't show every extreme that they name: `tile_rows`: row tile of each slot within the device's users. `tile_columns`: item tile of each slot within the step's item block; a device's slots of one step name distinct pairs of user tile and item tile, padding slots included. `tile_counts`: in every step some device uses all 64 slots.
All inputs are finite; a program needn't handle non-finite values.
Results may differ from a plain program's by a relative error of at most 0.0004.
Values may be sent and summed in bfloat16 or wider, within the bound.
A program may use at most 128 MiB of HBM per device.

v0:
```python
import jax
import jax.numpy as jnp
from jax import lax
from jax.sharding import PartitionSpec as P


def from_behind(block, axis, distance):
    devices = range(lax.axis_size(axis))
    route = [((i - distance) % len(devices), i) for i in devices]
    return lax.ppermute(block, axis, route)


def gradients(user_low, block_low, row_blocks, column_blocks, count, rating_tiles):
    tile_size = rating_tiles.shape[-1]
    factor_width = user_low.shape[1]
    row_tiles = user_low.shape[0] // tile_size
    item_tiles = block_low.shape[0] // tile_size
    slot_count = row_blocks.shape[0]
    user_tiles = user_low.reshape(row_tiles, tile_size, factor_width)[row_blocks]
    item_tiles_now = block_low.reshape(item_tiles, tile_size, factor_width)[column_blocks]
    predicted = jnp.einsum(
        "mik,mjk->mij", user_tiles, item_tiles_now, preferred_element_type=jnp.float32
    )
    in_list = jnp.arange(slot_count) < count
    observed = (rating_tiles > 0) & in_list[:, None, None]
    residual = jnp.where(observed, rating_tiles.astype(jnp.float32) - predicted, 0.0).astype(
        jnp.bfloat16
    )
    user_terms = jnp.einsum(
        "mij,mjk->mik", residual, item_tiles_now, preferred_element_type=jnp.float32
    )
    item_terms = jnp.einsum(
        "mij,mik->mjk", residual, user_tiles, preferred_element_type=jnp.float32
    )
    row_select = (row_blocks[:, None] == jnp.arange(row_tiles)[None, :]).astype(jnp.float32)
    column_select = (column_blocks[:, None] == jnp.arange(item_tiles)[None, :]).astype(jnp.float32)
    user_grad = jnp.einsum("mr,mik->rik", row_select, user_terms, precision=lax.Precision.HIGHEST)
    item_grad = jnp.einsum(
        "mr,mik->rik", column_select, item_terms, precision=lax.Precision.HIGHEST
    )
    return (user_grad.reshape(-1, factor_width), item_grad.reshape(-1, factor_width))


def shards(user_factors, item_factors, tile_rows, tile_columns, tile_counts, ratings):
    row_lists = tile_rows[0, 0]
    column_lists = tile_columns[0, 0]
    count_lists = tile_counts[0, 0]
    rating_lists = ratings[0, 0]
    step_total = rating_lists.shape[0]
    users_now = user_factors
    held_items = lax.all_gather(item_factors, "users", axis=0, tiled=True)
    for step_index in range(step_total):
        user_grad, item_grad = gradients(
            users_now.astype(jnp.bfloat16),
            held_items.astype(jnp.bfloat16),
            row_lists[step_index],
            column_lists[step_index],
            count_lists[step_index],
            rating_lists[step_index],
        )
        summed_grads = lax.psum(item_grad, "users")
        users_now = users_now + 0.01 * (user_grad - 0.05 * users_now)
        held_items = held_items + 0.003 * (summed_grads - 0.05 * held_items)
        if step_index < step_total - 1:
            held_items = from_behind(held_items, "strata", 1)
    own_rows = item_factors.shape[0]
    items_out = lax.dynamic_slice_in_dim(
        held_items, lax.axis_index("users") * own_rows, own_rows, 0
    )
    return (users_now, items_out)


def solution(mesh):
    placed = (
        P(("strata", "users"), None),
        P(("strata", "users"), None),
        P("strata", "users", None, None),
        P("strata", "users", None, None),
        P("strata", "users", None),
        P("strata", "users", None, None, None, None),
    )
    return jax.shard_map(
        shards,
        mesh=mesh,
        in_specs=placed,
        out_specs=(P(("strata", "users"), None), P(("strata", "users"), None)),
        check_vma=False,
    )
```

profile of v0, /device:TPU:1, one launch (start us, length us, event | category | flops | bytes accessed | tf_op | source)
XLA Modules:
  0.0 504.5 jit_solution(3911407407354205349)
XLA Ops:
  7.9 1.7 convert_element_type.36
  10.4 2.8 gather_fusion
  14.5 56.1 %all-gather.2.cloned.1.call-done = f32[1024,256]{1,0:T(8,128)} async-done(((f32[64,256]{1,0:T(8,128)}), f32[1024,256]{1,0:T(8,128)}) %all-gather.2.cloned.1.call-update) | async-done | bytes 1048592 | tf_op jit(solution)/shard_map/all_gather | solution.py:51
  70.6 1.3 convert_element_type.37
  71.9 2.8 gather_fusion.1
  74.7 6.1 %fusion.11 = bf16[64,128,128]{2,1,0:T(8,128)(2,1)S(1)} fusion(s32[1,1,2,64,128,128]{5,4,3,2,1,0:T(8,128)} %param.11, bf16[64,128,256]{2,1,0:T(8,128)(2,1)} %gather_fusion, bf16[64,128,256]{2,1,0:T(8,128)(2,1)} %gather_fusion.1, pred[64]{0:T(512)(128)(4,1)S(1)} %iota_compare_fusion.5), kind=kOutput, calls=%fused_computation.17 | convolution fusion | flops 543162368 | bytes 14680128 | tf_op jit(solution)/shard_map/mik,mjk->mij/dot_general | solution.py:21
  80.8 1.3 fusion.37
  82.1 7.5 %fusion.4 = f32[8,128,256]{2,0,1:T(8,128)S(1)} fusion(f32[64,128,256]{2,1,0:T(8,128)S(1)} %fusion.37, s32[64]{0:T(128)S(1)} %get-tuple-element.3), kind=kOutput, calls=%fused_computation.8 | convolution fusion | flops 201327104 | bytes 9437440 | tf_op jit(solution)/shard_map/mr,mik->rik/dot_general | solution.py:38
  89.6 1.3 copy.9
  90.9 12.9 %all-reduce.5.cloned.1.call-start = ((), (), s32[]{:S(2)}) async-start(), calls=%async_computation.2 | async-start | bytes 2097152 | tf_op jit(solution)/shard_map/psum | solution.py:61
  104.5 6.8 %fusion.36 = f32[64,128,256]{2,1,0:T(8,128)} fusion(bf16[64,128,128]{2,1,0:T(8,128)(2,1)S(1)} %fusion.11, bf16[64,128,256]{2,1,0:T(8,128)(2,1)} %gather_fusion.1), kind=kOutput, calls=%fused_computation.62 | convolution fusion | flops 536870912 | bytes 14680064 | tf_op jit(solution)/shard_map/mij,mjk->mik/dot_general | solution.py:29
  111.3 155.3 %all-reduce.3.cloned.1.call-done = f32[1024,256]{1,0:T(8,128)} async-done(((f32[1024,256]{1,0:T(8,128)}), f32[1024,256]{1,0:T(8,128)}) %all-reduce.3.cloned.1.call-update) | async-done | bytes 1048592 | tf_op jit(solution)/shard_map/psum | solution.py:61
  266.6 2.4 multiply_add_fusion
  269.0 1.4 collective-permute-start
  270.4 10.7 %fusion.6 = f32[16,128,256]{2,0,1:T(8,128)S(1)} fusion(f32[64,128,256]{2,1,0:T(8,128)} %fusion.36, s32[64]{0:T(128)S(1)} %get-tuple-element.5), kind=kOutput, calls=%fused_computation.10 | convolution fusion | flops 402654208 | bytes 10486016 | tf_op jit(solution)/shard_map/mr,mik->rik/dot_general | solution.py:37
  281.1 1.2 copy.8
  282.3 1.3 copy-done.4
  284.1 2.8 gather_fusion.2
  286.8 9.7 %collective-permute-done = f32[1024,256]{1,0:T(8,128)} collective-permute-done((f32[1024,256]{1,0:T(8,128)}, f32[1024,256]{1,0:T(8,128)}, u32[]{:S(2)}, u32[]{:S(2)}) %collective-permute-start) | collective-permute-done | bytes 1048608 | tf_op jit(solution)/shard_map/ppermute | solution.py:10
  296.5 1.3 convert_element_type.42
  297.8 2.8 gather_fusion.3
  300.6 6.1 %fusion.9 = bf16[64,128,128]{2,1,0:T(8,128)(2,1)S(1)} fusion(s32[1,1,2,64,128,128]{5,4,3,2,1,0:T(8,128)} %param.11, bf16[64,128,256]{2,1,0:T(8,128)(2,1)} %gather_fusion.2, bf16[64,128,256]{2,1,0:T(8,128)(2,1)} %gather_fusion.3, pred[64]{0:T(512)(128)(4,1)S(1)} %iota_compare_fusion.4), kind=kOutput, calls=%fused_computation.14 | convolution fusion | flops 543162368 | bytes 14680128 | tf_op jit(solution)/shard_map/mik,mjk->mij/dot_general | solution.py:21
  306.7 1.3 fusion.39
  308.0 0.9 copy-done.2
  308.9 4.5 fusion.38
  313.4 7.7 %fusion = f32[8,128,256]{2,0,1:T(8,128)S(1)} fusion(f32[64,128,256]{2,1,0:T(8,128)S(1)} %fusion.39, s32[64]{0:T(128)S(1)} %get-tuple-element.2), kind=kOutput, calls=%fused_computation.4 | convolution fusion | flops 201327104 | bytes 9437440 | tf_op jit(solution)/shard_map/mr,mik->rik/dot_general | solution.py:38
  321.0 1.3 copy.11
  322.4 10.7 %fusion.2 = f32[16,128,256]{2,0,1:T(8,128)S(1)} fusion(f32[64,128,256]{2,1,0:T(8,128)} %fusion.38, s32[64]{0:T(128)S(1)} %get-tuple-element.4), kind=kOutput, calls=%fused_computation.6 | convolution fusion | flops 402654208 | bytes 10486016 | tf_op jit(solution)/shard_map/mr,mik->rik/dot_general | solution.py:37
  333.1 1.2 copy.10
  334.7 1.9 fusion.13
  336.5 159.6 %all-reduce.5.cloned.1.call-done = f32[1024,256]{1,0:T(8,128)} async-done(((f32[1024,256]{1,0:T(8,128)}), f32[1024,256]{1,0:T(8,128)}) %all-reduce.5.cloned.1.call-update) | async-done | bytes 1048592 | tf_op jit(solution)/shard_map/psum | solution.py:61
  496.1 1.5 fusion.18
  (34 shorter events, 4.3 us)
Async XLA Ops:
  7.2 63.5 %all-gather.2.cloned.1.call-start = ((), (), s32[]{:S(2)}) async-start(), calls=%async_computation | async-start | bytes 1114112 | tf_op jit(solution)/shard_map/all_gather | solution.py:51
  7.9 258.7 %all-reduce.3.cloned.1.call-start = ((), (), s32[]{:S(2)}) async-start(), calls=%async_computation.1 | async-start | bytes 2097152 | tf_op jit(solution)/shard_map/psum | solution.py:61
  10.4 2.8 copy-start.9
  10.4 4.0 copy-start.7
  74.7 6.1 %copy-start = (bf16[64,128,256]{2,1,0:T(8,128)(2,1)S(1)}, bf16[64,128,256]{2,1,0:T(8,128)(2,1)}, u32[]{:S(2)}) copy-start(bf16[64,128,256]{2,1,0:T(8,128)(2,1)} %gather_fusion) | copy-start | bytes 12582916
  82.1 22.4 %copy-start.8 = (s32[1,1,2,64]{3,2,1,0:T(2,128)S(1)}, s32[1,1,2,64]{3,2,1,0:T(2,128)}, u32[]{:S(2)}) copy-start(s32[1,1,2,64]{3,2,1,0:T(2,128)} %param.8) | copy-start | bytes 1540
  90.9 405.2 %all-reduce.5.cloned.1.call-start = ((), (), s32[]{:S(2)}) async-start(), calls=%async_computation.2 | async-start | bytes 2097152 | tf_op jit(solution)/shard_map/psum | solution.py:61
  104.5 162.1 %copy-start.6 = (f32[1024,256]{1,0:T(8,128)S(1)}, f32[1024,256]{1,0:T(8,128)}, u32[]{:S(2)}) copy-start(f32[1024,256]{1,0:T(8,128)} %all-gather.2.cloned.1.call-done) | copy-start | bytes 3145732
  269.0 27.5 %collective-permute-start = (f32[1024,256]{1,0:T(8,128)}, f32[1024,256]{1,0:T(8,128)}, u32[]{:S(2)}, u32[]{:S(2)}) collective-permute-start(f32[1024,256]{1,0:T(8,128)} %multiply_add_fusion), channel_id=1, source_target_pairs={{240,0},{0,16},{16,32},{32,48},{48,64},{64,80},{80,96},{96,112},{1... | collective-permute-start | bytes 3145736 | tf_op jit(solution)/shard_map/ppermute | solution.py:10
  281.1 2.6 copy-start.3
  282.3 1.3 copy-start.4
  300.6 6.1 %copy-start.1 = (bf16[64,128,256]{2,1,0:T(8,128)(2,1)S(1)}, bf16[64,128,256]{2,1,0:T(8,128)(2,1)}, u32[]{:S(2)}) copy-start(bf16[64,128,256]{2,1,0:T(8,128)(2,1)} %gather_fusion.2) | copy-start | bytes 12582916
  306.7 2.2 copy-start.2
  333.1 1.6 copy-start.5
Sparse Core Ops, SparseCore 0:
  10.7 59.8 all-gather.1
  91.0 175.5 all-reduce.2
  322.5 173.5 all-reduce.4
where the time goes:
time: 513 us; the launch traced here: 505 us
  waiting for transfers between devices  381 us (74%)
  matrix products  62.6 us (12%)
  local copies, waits for them, and re-layouts  19.3 us (4%)
  between operations  14.4 us (3%)
  starting transfers between devices  14.3 us (3%)
  other arithmetic  12.5 us (2%)
    psum x2, waiting for transfers between devices, shards(): summed_grads = lax.psum(item_grad, 'users')  315 us
    all_gather x1, waiting for transfers between devices, shards(): held_items = lax.all_gather(item_factors, 'users', axis=0, tiled=True)  56.1 us
    dot_general x2, matrix products, gradients(): jnp.einsum('mr,mik->rik', row_select, user_terms, precision=lax.Precision...  21.4 us
    dot_general x2, matrix products, gradients(): jnp.einsum('mr,mik->rik', column_select, item_terms, precision=lax.Precis...  15.2 us
    psum x2, starting transfers between devices, shards(): summed_grads = lax.psum(item_grad, 'users')  12.9 us
    dot_general x2, matrix products, gradients(): jnp.einsum('mik,mjk->mij', user_tiles, item_tiles_now, preferred_element_...  12.2 us
    dot_general x2, matrix products, gradients(): jnp.einsum('mij,mjk->mik', residual, item_tiles_now, preferred_element_ty...  11.3 us
  transfers between devices with their start and end apart: 4, of which 4 were waited for; matrix products, arithmetic and copies ran while one was open for 8% of the time, Pallas kernels for 0%

commit v1 on v0

--- a/solution.py
+++ b/solution.py
@@ -48,7 +48,9 @@
     rating_lists = ratings[0, 0]
     step_total = rating_lists.shape[0]
     users_now = user_factors
-    held_items = lax.all_gather(item_factors, "users", axis=0, tiled=True)
+    held_items = jnp.concatenate(
+        lax.all_to_all(jnp.stack([item_factors] * lax.axis_size("users")), "users", 0, 0), axis=0
+    )
     for step_index in range(step_total):
         user_grad, item_grad = gradients(
             users_now.astype(jnp.bfloat16),

time: 513 us -> 497 us (0.969)
  waiting for transfers between devices: 381 us -> 352 us
  starting transfers between devices: 14.3 us -> 26.9 us
    all_gather x1 -> x0, waiting for transfers between devices: 56.1 us -> none  [shards(): held_items = lax.all_gather(item_factors, 'users', axis=0, tiled=True)]
    all_to_all x0 -> x1, waiting for transfers between devices: none -> 17.8 us  [shards(): lax.all_to_all(jnp.stack([item_factors] * lax.axis_size('users')), 'users...]
    all_to_all x0 -> x1, starting transfers between devices: none -> 12.6 us  [shards(): lax.all_to_all(jnp.stack([item_factors] * lax.axis_size('users')), 'users...]
    psum x2, waiting for transfers between devices: 315 us -> 324 us  [shards(): summed_grads = lax.psum(item_grad, 'users')]
where the time goes in v1:
time: 497 us; the launch traced here: 488 us
  waiting for transfers between devices  352 us (71%)
  matrix products  62.4 us (13%)
  starting transfers between devices  26.9 us (5%)
  local copies, waits for them, and re-layouts  21.4 us (4%)
  between operations  14.7 us (3%)
  other arithmetic  10.5 us (2%)
    psum x2, waiting for transfers between devices, shards(): summed_grads = lax.psum(item_grad, 'users')  324 us
    dot_general x2, matrix products, gradients(): jnp.einsum('mr,mik->rik', row_select, user_terms, precision=lax.Precision...  21.4 us
    all_to_all x1, waiting for transfers between devices, shards(): lax.all_to_all(jnp.stack([item_factors] * lax.axis_size('users')), 'users...  17.8 us
    dot_general x2, matrix products, gradients(): jnp.einsum('mr,mik->rik', column_select, item_terms, precision=lax.Precis...  15.2 us
    psum x2, starting transfers between devices, shards(): summed_grads = lax.psum(item_grad, 'users')  12.9 us
    all_to_all x1, starting transfers between devices, shards(): lax.all_to_all(jnp.stack([item_factors] * lax.axis_size('users')), 'users...  12.6 us
    dot_general x2, matrix products, gradients(): jnp.einsum('mik,mjk->mij', user_tiles, item_tiles_now, preferred_element_...  12.2 us
    dot_general x2, matrix products, gradients(): jnp.einsum('mij,mjk->mik', residual, item_tiles_now, preferred_element_ty...  11.1 us
  transfers between devices with their start and end apart: 4, of which 4 were waited for; matrix products, arithmetic and copies ran while one was open for 8% of the time, Pallas kernels for 0%

profile of v1, /device:TPU:1, one launch (start us, length us, event | category | flops | bytes accessed | tf_op | source)
XLA Modules:
  0.0 487.6 jit_solution(10158579715231001767)
XLA Ops:
  7.2 2.1 stack.2
  9.3 12.6 %all-to-all-start = ((f32[16,64,256]{2,1,0:T(8,128)}), f32[16,64,256]{2,1,0:T(8,128)}, u32[]{:S(2)}, u32[]{:S(2)}) async-start(f32[16,64,256]{2,1,0:T(8,128)} %stack.2), calls=%async_computation | async-start | bytes 2097152 | tf_op jit(solution)/shard_map/all_to_all | solution.py:52
  22.1 2.8 gather_fusion
  26.1 17.8 %all-to-all-done = f32[16,64,256]{2,1,0:T(8,128)} async-done(((f32[16,64,256]{2,1,0:T(8,128)}), f32[16,64,256]{2,1,0:T(8,128)}, u32[]{:S(2)}, u32[]{:S(2)}) %all-to-all-start) | async-done | bytes 1048608 | tf_op jit(solution)/shard_map/all_to_all | solution.py:52
  43.9 1.3 convert_element_type.41
  45.2 2.8 gather_fusion.1
  48.0 6.1 %fusion.11 = bf16[64,128,128]{2,1,0:T(8,128)(2,1)S(1)} fusion(s32[1,1,2,64,128,128]{5,4,3,2,1,0:T(8,128)} %param.11, bf16[64,128,256]{2,1,0:T(8,128)(2,1)} %gather_fusion, bf16[64,128,256]{2,1,0:T(8,128)(2,1)} %gather_fusion.1, pred[64]{0:T(512)(128)(4,1)S(1)} %iota_compare_fusion.5), kind=kOutput, calls=%fused_computation.17 | convolution fusion | flops 543162368 | bytes 14680128 | tf_op jit(solution)/shard_map/mik,mjk->mij/dot_general | solution.py:21
  54.1 1.3 fusion.39
  55.4 7.5 %fusion.4 = f32[8,128,256]{2,0,1:T(8,128)S(1)} fusion(f32[64,128,256]{2,1,0:T(8,128)S(1)} %fusion.39, s32[64]{0:T(128)S(1)} %get-tuple-element.3), kind=kOutput, calls=%fused_computation.8 | convolution fusion | flops 201327104 | bytes 9437440 | tf_op jit(solution)/shard_map/mr,mik->rik/dot_general | solution.py:38
  62.9 1.3 copy.9
  64.2 12.9 %all-reduce.5.cloned.1.call-start = ((), (), s32[]{:S(2)}) async-start(), calls=%async_computation.2 | async-start | bytes 2097152 | tf_op jit(solution)/shard_map/psum | solution.py:63
  77.8 6.7 %fusion.38 = f32[64,128,256]{2,1,0:T(8,128)} fusion(bf16[64,128,128]{2,1,0:T(8,128)(2,1)S(1)} %fusion.11, bf16[64,128,256]{2,1,0:T(8,128)(2,1)} %gather_fusion.1), kind=kOutput, calls=%fused_computation.65 | convolution fusion | flops 536870912 | bytes 14680064 | tf_op jit(solution)/shard_map/mij,mjk->mik/dot_general | solution.py:29
  84.5 164.3 %all-reduce.3.cloned.1.call-done = f32[1024,256]{1,0:T(8,128)} async-done(((f32[1024,256]{1,0:T(8,128)}), f32[1024,256]{1,0:T(8,128)}) %all-reduce.3.cloned.1.call-update) | async-done | bytes 1048592 | tf_op jit(solution)/shard_map/psum | solution.py:63
  248.8 2.7 bitcast_add_fusion
  251.4 1.4 collective-permute-start
  252.8 10.7 %fusion.6 = f32[16,128,256]{2,0,1:T(8,128)S(1)} fusion(f32[64,128,256]{2,1,0:T(8,128)} %fusion.38, s32[64]{0:T(128)S(1)} %get-tuple-element.5), kind=kOutput, calls=%fused_computation.10 | convolution fusion | flops 402654208 | bytes 10486016 | tf_op jit(solution)/shard_map/mr,mik->rik/dot_general | solution.py:37
  263.5 1.2 copy.8
  264.8 1.3 copy-done.5
  266.5 2.8 gather_fusion.2
  269.3 9.7 %collective-permute-done = f32[1024,256]{1,0:T(8,128)} collective-permute-done((f32[1024,256]{1,0:T(8,128)}, f32[1024,256]{1,0:T(8,128)}, u32[]{:S(2)}, u32[]{:S(2)}) %collective-permute-start) | collective-permute-done | bytes 1048608 | tf_op jit(solution)/shard_map/ppermute | solution.py:10
  279.0 1.3 convert_element_type.47
  280.3 2.8 gather_fusion.3
  283.1 6.1 %fusion.9 = bf16[64,128,128]{2,1,0:T(8,128)(2,1)S(1)} fusion(s32[1,1,2,64,128,128]{5,4,3,2,1,0:T(8,128)} %param.11, bf16[64,128,256]{2,1,0:T(8,128)(2,1)} %gather_fusion.2, bf16[64,128,256]{2,1,0:T(8,128)(2,1)} %gather_fusion.3, pred[64]{0:T(512)(128)(4,1)S(1)} %iota_compare_fusion.4), kind=kOutput, calls=%fused_computation.14 | convolution fusion | flops 543162368 | bytes 14680128 | tf_op jit(solution)/shard_map/mik,mjk->mij/dot_general | solution.py:21
  289.2 1.3 fusion.41
  291.3 4.5 fusion.40
  295.8 7.7 %fusion = f32[8,128,256]{2,0,1:T(8,128)S(1)} fusion(f32[64,128,256]{2,1,0:T(8,128)S(1)} %fusion.41, s32[64]{0:T(128)S(1)} %get-tuple-element.2), kind=kOutput, calls=%fused_computation.4 | convolution fusion | flops 201327104 | bytes 9437440 | tf_op jit(solution)/shard_map/mr,mik->rik/dot_general | solution.py:38
  303.5 1.3 copy.11
  304.8 10.7 %fusion.2 = f32[16,128,256]{2,0,1:T(8,128)S(1)} fusion(f32[64,128,256]{2,1,0:T(8,128)} %fusion.40, s32[64]{0:T(128)S(1)} %get-tuple-element.4), kind=kOutput, calls=%fused_computation.6 | convolution fusion | flops 402654208 | bytes 10486016 | tf_op jit(solution)/shard_map/mr,mik->rik/dot_general | solution.py:37
  315.5 1.2 copy.10
  317.1 1.9 fusion.13
  319.0 159.9 %all-reduce.5.cloned.1.call-done = f32[1024,256]{1,0:T(8,128)} async-done(((f32[1024,256]{1,0:T(8,128)}), f32[1024,256]{1,0:T(8,128)}) %all-reduce.5.cloned.1.call-update) | async-done | bytes 1048592 | tf_op jit(solution)/shard_map/psum | solution.py:63
  478.8 1.5 fusion.20
  (34 shorter events, 3.8 us)
Async XLA Ops:
  7.2 14.7 %copy-start.3 = (f32[2048,256]{1,0:T(8,128)S(1)}, f32[2048,256]{1,0:T(8,128)}, u32[]{:S(2)}) copy-start(f32[2048,256]{1,0:T(8,128)} %param.6) | copy-start | bytes 6291460
  7.2 14.9 %copy-start.8 = (s32[1,1,2,64]{3,2,1,0:T(2,128)S(1)}, s32[1,1,2,64]{3,2,1,0:T(2,128)}, u32[]{:S(2)}) copy-start(s32[1,1,2,64]{3,2,1,0:T(2,128)} %param.8) | copy-start | bytes 1540
  7.2 14.9 %copy-start.7 = (s32[1,1,2,64]{3,2,1,0:T(2,128)S(1)}, s32[1,1,2,64]{3,2,1,0:T(2,128)}, u32[]{:S(2)}) copy-start(s32[1,1,2,64]{3,2,1,0:T(2,128)} %param.9) | copy-start | bytes 1540
  9.3 34.7 %all-to-all-start = ((f32[16,64,256]{2,1,0:T(8,128)}), f32[16,64,256]{2,1,0:T(8,128)}, u32[]{:S(2)}, u32[]{:S(2)}) async-start(f32[16,64,256]{2,1,0:T(8,128)} %stack.2), calls=%async_computation | async-start | bytes 2097152 | tf_op jit(solution)/shard_map/all_to_all | solution.py:52
  21.9 226.9 %all-reduce.3.cloned.1.call-start = ((), (), s32[]{:S(2)}) async-start(), calls=%async_computation.1 | async-start | bytes 2097152 | tf_op jit(solution)/shard_map/psum | solution.py:63
  22.1 2.8 copy-start.9
  48.0 6.1 %copy-start = (bf16[64,128,256]{2,1,0:T(8,128)(2,1)S(1)}, bf16[64,128,256]{2,1,0:T(8,128)(2,1)}, u32[]{:S(2)}) copy-start(bf16[64,128,256]{2,1,0:T(8,128)(2,1)} %gather_fusion) | copy-start | bytes 12582916
  64.2 414.6 %all-reduce.5.cloned.1.call-start = ((), (), s32[]{:S(2)}) async-start(), calls=%async_computation.2 | async-start | bytes 2097152 | tf_op jit(solution)/shard_map/psum | solution.py:63
  251.4 27.5 %collective-permute-start = (f32[1024,256]{1,0:T(8,128)}, f32[1024,256]{1,0:T(8,128)}, u32[]{:S(2)}, u32[]{:S(2)}) collective-permute-start(f32[1024,256]{1,0:T(8,128)} %bitcast_add_fusion), channel_id=1, source_target_pairs={{240,0},{0,16},{16,32},{32,48},{48,64},{64,80},{80,96},{96,112},{1... | collective-permute-start | bytes 3145736 | tf_op jit(solution)/shard_map/ppermute | solution.py:10
  263.5 2.6 copy-start.4
  264.8 1.3 copy-start.5
  283.1 6.1 %copy-start.1 = (bf16[64,128,256]{2,1,0:T(8,128)(2,1)S(1)}, bf16[64,128,256]{2,1,0:T(8,128)(2,1)}, u32[]{:S(2)}) copy-start(bf16[64,128,256]{2,1,0:T(8,128)(2,1)} %gather_fusion.2) | copy-start | bytes 12582916
  289.1 2.2 copy-start.2
  315.5 1.6 copy-start.6
Sparse Core Ops, SparseCore 0:
  64.3 184.3 all-reduce.2
  304.9 173.8 all-reduce.4
